TPU v7x, 32 devices: a whole 2x2x4 slice. The times are simulated.
32 devices in a mesh: groups: 2 (over x), row: 16 (over z, y, core).
Axes of the slice: x: 2, y: 2, z: 4, core: 2. Of those that a mesh axis runs over, the one named last changes fastest.
Arguments:
- features: bfloat16 [128, 64, 512], P(('groups', 'row')), parts along dimension 0, may hold values from -6 to 6
- cotangent: bfloat16 [128, 64, 512], P(('groups', 'row')), parts along dimension 0, may hold values from -6 to 6
- depth_weight: bfloat16 [49, 512], P(None, 'row'), may hold values from -0.875 to 0.875
- depth_bias: bfloat16 [512], P('row'), may hold values from -3 to 3
- norm_gain: bfloat16 [512], P('row'), may hold values from 0.25 to 1.75
- norm_shift: bfloat16 [512], P('row'), may hold values from -3 to 3
- up_weight: bfloat16 [512, 2048], P('row'), may hold values from -0.25 to 0.25
- up_bias: bfloat16 [2048], P('row'), may hold values from -3 to 3
- down_weight: bfloat16 [2048, 512], P('row'), may hold values from -0.125 to 0.125
- down_bias: bfloat16 [512], P('row'), may hold values from -3 to 3
Outputs:
- block_out: bfloat16 [128, 64, 512], P(('groups', 'row')), parts along dimension 0
- grad_features: bfloat16 [128, 64, 512], P(('groups', 'row')), parts along dimension 0
- grad_up_weight: float32 [1024, 2048], P(('groups', 'row')), parts along dimension 0
- grad_down_weight: float32 [4096, 512], P(('groups', 'row')), parts along dimension 0
- grad_depth_weight: float32 [98, 512], P('groups', 'row'), parts along dimension 0
- grad_depth_bias: float32 [1024], P(('groups', 'row')), parts along dimension 0
- grad_norm_gain: float32 [1024], P(('groups', 'row')), parts along dimension 0
- grad_norm_shift: float32 [1024], P(('groups', 'row')), parts along dimension 0
- grad_up_bias: float32 [4096], P(('groups', 'row')), parts along dimension 0
- grad_down_bias: float32 [1024], P(('groups', 'row')), parts along dimension 0
There are 2 independent parts, one for each index of `groups`. A program takes and returns all parts, laid end to end along the dimension named above; an argument that names none is the same for every part. Nothing has to cross between parts.
All inputs are finite; a program needn't handle non-finite values.
Results may differ from a plain program's by a relative error of at most 0.0055.
Values may be sent and summed in bfloat16 or wider, within the bound.
A program may use at most 64 MiB of HBM per device.

v0:
```python
import math
import jax
import jax.numpy as jnp
from jax import lax
from jax.sharding import PartitionSpec as P

eps = 1e-06


def with_halo(block, sides, width):
    for axis, dim in sides:
        count = lax.axis_size(axis)
        forward = [(i, i + 1) for i in range(count - 1)]
        backward = [(target, source) for source, target in forward]
        low = lax.ppermute(
            lax.slice_in_dim(block, block.shape[dim] - width, None, axis=dim), axis, forward
        )
        high = lax.ppermute(lax.slice_in_dim(block, 0, width, axis=dim), axis, backward)
        block = jnp.concatenate([low, block, high], axis=dim)
    return block


def gelu_value(value):
    return 0.5 * value * (1.0 + lax.erf(value * (1.0 / math.sqrt(2.0))))


def gelu_slope(value):
    cumulative = 0.5 * (1.0 + lax.erf(value * (1.0 / math.sqrt(2.0))))
    density = jnp.exp(-0.5 * value * value) * (1.0 / math.sqrt(2.0 * math.pi))
    return cumulative + value * density


def depth_conv(padded, kernel, height, width):
    total = jnp.zeros((height, width, kernel.shape[1]), jnp.float32)
    for first in range(7):
        for second in range(7):
            total = (
                total
                + padded[first : first + height, second : second + width, :]
                * kernel[first * 7 + second]
            )
    return total


def depth_conv_back(padded, kernel, height, width):
    total = jnp.zeros((height, width, kernel.shape[1]), jnp.float32)
    for first in range(7):
        for second in range(7):
            total = (
                total
                + padded[6 - first : 6 - first + height, 6 - second : 6 - second + width, :]
                * kernel[first * 7 + second]
            )
    return total


def per_device(
    features,
    cotangent,
    depth_weight,
    depth_bias,
    norm_gain,
    norm_shift,
    up_weight,
    up_bias,
    down_weight,
    down_bias,
):
    height, width, chans = features.shape
    devices = lax.axis_size("row")
    cells = height * width
    scale = 1.0 / math.sqrt(cells * devices)
    kernel, conv_bias, gain, shift, bias_down, bias_up = (
        lax.all_gather(depth_weight, "row", axis=1, tiled=True),
        lax.all_gather(depth_bias, "row", axis=0, tiled=True),
        lax.all_gather(norm_gain, "row", axis=0, tiled=True),
        lax.all_gather(norm_shift, "row", axis=0, tiled=True),
        lax.all_gather(down_bias, "row", axis=0, tiled=True),
        lax.all_gather(up_bias, "row", axis=0, tiled=True),
    )
    kernel = kernel.astype(jnp.float32)
    gain = gain.astype(jnp.float32)
    rimmed = with_halo(features, (("row", 0),), 3)
    padded = jnp.pad(rimmed.astype(jnp.float32), ((0, 0), (3, 3), (0, 0)))
    conv = depth_conv(padded, kernel, height, width) + conv_bias.astype(jnp.float32)
    mean_val = jnp.mean(conv, axis=2, keepdims=True)
    centered = conv - mean_val
    var_val = jnp.mean(centered * centered, axis=2, keepdims=True)
    inv = lax.rsqrt(var_val + eps)
    normed = centered * inv
    normal_out = (normed * gain + shift.astype(jnp.float32)).astype(jnp.bfloat16)
    flat_norm = normal_out.reshape(cells, chans)
    flat_cot = cotangent.reshape(cells, chans)
    columns = flat_norm
    hidden = jnp.dot(
        columns,
        lax.all_gather(up_weight, "row", axis=0, tiled=True),
        preferred_element_type=jnp.float32,
    ) + bias_up.astype(jnp.float32)
    act = gelu_value(hidden).astype(jnp.bfloat16)
    columns = act
    mixed = jnp.dot(
        columns,
        lax.all_gather(down_weight, "row", axis=0, tiled=True),
        preferred_element_type=jnp.float32,
    )
    block_out = (
        features.astype(jnp.float32)
        + (mixed + bias_down.astype(jnp.float32)).reshape(height, width, chans)
    ).astype(jnp.bfloat16)
    down_full = (
        lax.dot_general(act, flat_cot, (((0,), (0,)), ((), ())), preferred_element_type=jnp.float32)
        * scale
    )
    grad_down_weight = lax.psum_scatter(down_full, "row", scatter_dimension=0, tiled=True)
    dact = lax.dot_general(
        flat_cot,
        lax.all_gather(down_weight, "row", axis=0, tiled=True),
        (((1,), (1,)), ((), ())),
        preferred_element_type=jnp.float32,
    )
    dhidden = (dact * gelu_slope(hidden)).astype(jnp.bfloat16)
    columns = flat_norm
    grad_up_weight = lax.psum_scatter(
        lax.dot_general(
            columns, dhidden, (((0,), (0,)), ((), ())), preferred_element_type=jnp.float32
        )
        * scale,
        "row",
        scatter_dimension=0,
        tiled=True,
    )
    dnorm = lax.dot_general(
        dhidden,
        lax.all_gather(up_weight, "row", axis=0, tiled=True),
        (((1,), (1,)), ((), ())),
        preferred_element_type=jnp.float32,
    )
    dnorm = dnorm.reshape(height, width, chans)
    down_bias_term = jnp.sum(flat_cot.astype(jnp.float32), axis=0) * scale
    up_bias_term = jnp.sum(dhidden.astype(jnp.float32), axis=0) * scale
    gain_term = jnp.sum(dnorm * normed, axis=(0, 1)) * scale
    shift_term = jnp.sum(dnorm, axis=(0, 1)) * scale
    grad_down_bias, grad_up_bias, grad_norm_gain, grad_norm_shift = (
        lax.psum_scatter(down_bias_term, "row", scatter_dimension=0, tiled=True),
        lax.psum_scatter(up_bias_term, "row", scatter_dimension=0, tiled=True),
        lax.psum_scatter(gain_term, "row", scatter_dimension=0, tiled=True),
        lax.psum_scatter(shift_term, "row", scatter_dimension=0, tiled=True),
    )
    scaled = dnorm * gain
    dconv = inv * (
        scaled
        - jnp.mean(scaled, axis=2, keepdims=True)
        - normed * jnp.mean(scaled * normed, axis=2, keepdims=True)
    )
    dconv = dconv.astype(jnp.bfloat16)
    dconv_wide = dconv.astype(jnp.float32)
    back_rim = with_halo(dconv, (("row", 0),), 3)
    back_pad = jnp.pad(back_rim.astype(jnp.float32), ((0, 0), (3, 3), (0, 0)))
    grad_features = (
        cotangent.astype(jnp.float32) + depth_conv_back(back_pad, kernel, height, width)
    ).astype(jnp.bfloat16)
    taps = []
    for first in range(7):
        for second in range(7):
            taps.append(
                jnp.sum(
                    dconv_wide * padded[first : first + height, second : second + width, :],
                    axis=(0, 1),
                )
            )
    kernel_term = jnp.stack(taps, axis=0) * scale
    conv_bias_term = jnp.sum(dconv_wide, axis=(0, 1)) * scale
    grad_depth_weight, grad_depth_bias = (
        lax.psum_scatter(kernel_term, "row", scatter_dimension=1, tiled=True),
        lax.psum_scatter(conv_bias_term, "row", scatter_dimension=0, tiled=True),
    )
    return (
        block_out,
        grad_features,
        grad_up_weight,
        grad_down_weight,
        grad_depth_weight,
        grad_depth_bias,
        grad_norm_gain,
        grad_norm_shift,
        grad_up_bias,
        grad_down_bias,
    )


def solution(mesh):
    placed = (
        P(("groups", "row"), None, None),
        P(("groups", "row"), None, None),
        P(None, "row"),
        P("row"),
        P("row"),
        P("row"),
        P("row", None),
        P("row"),
        P("row", None),
        P("row"),
    )
    return jax.shard_map(
        per_device,
        mesh=mesh,
        in_specs=placed,
        out_specs=(
            P(("groups", "row"), None, None),
            P(("groups", "row"), None, None),
            P(("groups", "row"), None),
            P(("groups", "row"), None),
            P("groups", "row"),
            P(("groups", "row")),
            P(("groups", "row")),
            P(("groups", "row")),
            P(("groups", "row")),
            P(("groups", "row")),
        ),
        check_vma=False,
    )
```

profile of v0, /device:TPU:0, one launch (start us, length us, event | category | flops | bytes accessed | tf_op | source)
XLA Modules:
  0.0 336.8 jit_solution(5923359344454385601)
XLA Ops:
  9.8 2.4 collective-permute-start
  12.2 1.3 collective-permute-start.1
  13.5 25.6 %all_gather.26 = bf16[49,512]{0,1:T(8,128)(2,1)S(1)} all-gather(bf16[49,32]{0,1:T(8,128)(2,1)} %param.12), channel_id=1, replica_groups=mesh['groups'=2,'row'=16] {'row'}, dimensions={1}, use_global_device_ids=true | all-gather | bytes 53312 | tf_op jit(solution)/shard_map/all_gather | solution.py:74
  39.1 2.6 slice_reduce_fusion.48
  41.8 1.6 slice_reduce_fusion.46
  45.7 30.5 %all-reduce.12 = (bf16[512]{0:T(512)(128)(2,1)S(1)}, bf16[512]{0:T(512)(128)(2,1)S(1)}, bf16[512]{0:T(512)(128)(2,1)S(1)}, bf16[512]{0:T(512)(128)(2,1)}) all-reduce(bf16[512]{0:T(512)(128)(2,1)S(1)} %dynamic-update-slice, bf16[512]{0:T(512)(128)(2,1)S(1)} %dynamic-update-slice.2, ...), channel_id=1, replica_groups=mesh['groups'=2,'row'=16] {'row'}, use_global_device_ids=true, to_apply=%add.2 | all-reduce | flops 2048 | bytes 8192
  76.2 17.5 %all-gather = bf16[16,1,128]{2,1,0:T(2,128)(2,1)S(1)} all-gather(bf16[1,1,128]{2,1,0:T(2,128)(2,1)S(1)} %bitcast.131), channel_id=1, replica_groups=mesh['groups'=2,'row'=16] {'row'}, dimensions={0}, use_global_device_ids=true | all-gather | bytes 4352 | tf_op jit(solution)/shard_map/all_gather | solution.py:79
  93.8 2.7 slice_reduce_fusion.47
  96.8 4.7 %fusion.146 = (f32[4,64]{1,0:T(4,128)S(1)}, f32[4,64,512]{2,1,0:T(8,128)S(1)}) fusion(f32[512]{0:T(512)S(1)} %convert_element_type.62, f32[512]{0:T(512)S(1)} %get-tuple-element.85, f32[512]{0:T(512)S(1)} %get-tuple-element.86, f32[512]{0:T(512)S(1)} %get-tuple-element.87, f32[512]{0:T(512)S(1)} %get-tuple-element.88, ...), kind=kLoop, calls=%fused_computation.368 | loop fusion | flops 12975872 | bytes 5608448 | tf_op jit(solution)/shard_map/reduce_sum | solution.py:86
  102.1 3.8 %multiply_convert_fusion = (bf16[256,2048]{1,0:T(8,128)(2,1)S(1)}, f32[256,2048]{1,0:T(8,128)}) fusion(f32[2048]{0:T(1024)S(1)} %bitcast.81, bf16[256,512]{1,0:T(8,128)(2,1)S(1)} %bitcast.75, bf16[512,2048]{1,0:T(8,128)(2,1)} %all-gather.4.cloned.1.call-done), kind=kOutput, calls=%fused_computation.61 | convolution fusion | flops 540016640 | bytes 5513216 | tf_op jit(solution)/shard_map/dot_general | solution.py:95
  106.0 4.2 %convert_reduce_fusion.1 = (f32[2048]{0:T(1024)}, bf16[256,2048]{1,0:T(8,128)(2,1)S(1)}) fusion(f32[256,2048]{1,0:T(8,128)} %get-tuple-element.152, bf16[256,512]{1,0:T(8,128)(2,1)} %bitcast.77, bf16[2048,512]{1,0:T(8,128)(2,1)} %all-gather.6.cloned.1.call-done), kind=kOutput, calls=%fused_computation.60 | convolution fusion | flops 543160320 | bytes 5513216 | tf_op jit(solution)/shard_map/dot_general | solution.py:116
  110.2 1.3 fusion.145
  114.4 3.2 fusion.143
  117.5 1.4 fusion.142
  120.3 2.3 stack.199
  123.8 3.9 %convolution_multiply_fusion.1 = f32[512,2048]{1,0:T(8,128)} fusion(bf16[256,512]{1,0:T(8,128)(2,1)S(1)} %bitcast.76, bf16[256,2048]{1,0:T(8,128)(2,1)} %copy-done.6), kind=kOutput, calls=%fused_computation.51 | convolution fusion | flops 537919488 | bytes 5505024 | tf_op jit(solution)/shard_map/dot_general | solution.py:125
  128.6 2.7 convolution_multiply_fusion
  132.8 59.3 %all-reduce.11 = (f32[512]{0:T(512)S(1)}, f32[512]{0:T(512)S(1)}, f32[512]{0:T(512)S(1)}, f32[2048]{0:T(1024)S(1)}, f32[512]{0:T(512)S(1)}) all-reduce(f32[512]{0:T(512)S(1)} %broadcast_multiply_fusion.5, f32[512]{0:T(512)S(1)} %get-tuple-element.157, ...), channel_id=5, replica_groups=mesh['groups'=2,'row'=16] {'row'}, use_global_device_ids=true, to_apply=%region_57.58.clone | all-reduce | flops 4096 | bytes 32768
  194.5 1.3 collective-permute-start.2
  195.8 1.3 collective-permute-start.3
  197.7 2.4 convolution_add_fusion.1
  201.4 4.7 %fusion.5 = bf16[4,64,512]{2,1,0:T(8,128)(2,1)} fusion(bf16[4,64,512]{2,1,0:T(8,128)(2,1)S(1)} %copy-done.4, f32[10,64,512]{2,1,0:T(8,128)S(1)} %maximum_convert_fusion.1, f32[512]{0:T(512)S(1)} %get-tuple-element.85, f32[512]{0:T(512)S(1)} %get-tuple-element.86, f32[512]{0:T(512)S(1)} %get-tuple-element.87, f32[512]{0:T(512)S(1)} %get-tuple-element.88, ...), kind=kLoop, calls=%fused_computation.152 | loop fusion | flops 13107200 | bytes 5605376 | tf_op jit(solution)/shard_map/convert_element_type | solution.py:162
  206.0 48.2 %reduce-scatter.6.cloned.1.call-done = f32[32,2048]{1,0:T(8,128)} async-done(((f32[512,2048]{1,0:T(8,128)}), f32[32,2048]{1,0:T(8,128)}) %reduce-scatter.6.cloned.1.call-update) | async-done | bytes 262160 | tf_op jit(solution)/shard_map/reduce_scatter | solution.py:124
  254.2 76.1 %reduce-scatter.8.cloned.1.call-done = f32[128,512]{1,0:T(8,128)} async-done(((f32[2048,512]{1,0:T(8,128)}), f32[128,512]{1,0:T(8,128)}) %reduce-scatter.8.cloned.1.call-update) | async-done | bytes 262160 | tf_op jit(solution)/shard_map/reduce_scatter | solution.py:115
  (198 shorter events, 14.9 us)
Async XLA Ops:
  7.2 94.9 %all-gather.4.cloned.1.call-start = ((), (), s32[]{:S(2)}) async-start(), calls=%async_computation.3 | async-start | bytes 2228224 | tf_op jit(solution)/shard_map/all_gather | solution.py:97
  7.9 98.0 %all-gather.6.cloned.1.call-start = ((), (), s32[]{:S(2)}) async-start(), calls=%async_computation.4 | async-start | bytes 2228224 | tf_op jit(solution)/shard_map/all_gather | solution.py:104
  8.7 197.4 %reduce-scatter.10.cloned.1.call-start = ((), (), s32[]{:S(2)}) async-start(), calls=%async_computation.7 | async-start | bytes 278528
  9.8 86.9 %collective-permute-start = (bf16[3,64,512]{2,1,0:T(8,128)(2,1)S(1)}, bf16[3,64,512]{2,1,0:T(8,128)(2,1)S(1)}, u32[]{:S(2)}, u32[]{:S(2)}) collective-permute-start(bf16[3,64,512]{2,1,0:T(8,128)(2,1)S(1)} %get-tuple-element.147), channel_id=1, source_target_pairs={{0,1},{1,2},{2,3},{3,4},{4,5},{5,6},{6,7},{7,8},{8,9},{9,10},{10,1... | collective-permute-start | bytes 589832 | tf_op jit(solution)/shard_map/ppermute | solution.py:15
  12.2 84.5 %collective-permute-start.1 = (bf16[3,64,512]{2,1,0:T(8,128)(2,1)S(1)}, bf16[3,64,512]{2,1,0:T(8,128)(2,1)S(1)}, u32[]{:S(2)}, u32[]{:S(2)}) collective-permute-start(bf16[3,64,512]{2,1,0:T(8,128)(2,1)S(1)} %get-tuple-element.148), channel_id=1, source_target_pairs={{1,0},{2,1},{3,2},{4,3},{5,4},{6,5},{7,6},{8,7},{9,8},{10,9},{11,1... | collective-permute-start | bytes 589832 | tf_op jit(solution)/shard_map/ppermute | solution.py:18
  41.8 34.4 %copy-start.65 = (bf16[128]{0:T(256)(128)(2,1)S(1)}, bf16[128]{0:T(256)(128)(2,1)}, u32[]{:S(2)}) copy-start(bf16[128]{0:T(256)(128)(2,1)} %param.17) | copy-start | bytes 772
  96.5 5.0 %copy-start.7 = (f32[512]{0:T(512)}, f32[512]{0:T(512)S(1)}, u32[]{:S(2)}) copy-start(f32[512]{0:T(512)S(1)} %get-tuple-element.104) | copy-start | bytes 6148
  96.5 5.0 %copy-start.9 = (f32[512]{0:T(512)}, f32[512]{0:T(512)S(1)}, u32[]{:S(2)}) copy-start(f32[512]{0:T(512)S(1)} %get-tuple-element.105) | copy-start | bytes 6148
  96.5 5.0 %copy-start.11 = (f32[512]{0:T(512)}, f32[512]{0:T(512)S(1)}, u32[]{:S(2)}) copy-start(f32[512]{0:T(512)S(1)} %get-tuple-element.106) | copy-start | bytes 6148
  96.5 5.0 %copy-start.13 = (f32[512]{0:T(512)}, f32[512]{0:T(512)S(1)}, u32[]{:S(2)}) copy-start(f32[512]{0:T(512)S(1)} %get-tuple-element.107) | copy-start | bytes 6148
  96.5 5.0 %copy-start.15 = (f32[512]{0:T(512)}, f32[512]{0:T(512)S(1)}, u32[]{:S(2)}) copy-start(f32[512]{0:T(512)S(1)} %get-tuple-element.108) | copy-start | bytes 6148
  96.5 5.0 %copy-start.17 = (f32[512]{0:T(512)}, f32[512]{0:T(512)S(1)}, u32[]{:S(2)}) copy-start(f32[512]{0:T(512)S(1)} %get-tuple-element.109) | copy-start | bytes 6148
  96.5 5.0 %copy-start.19 = (f32[512]{0:T(512)}, f32[512]{0:T(512)S(1)}, u32[]{:S(2)}) copy-start(f32[512]{0:T(512)S(1)} %get-tuple-element.110) | copy-start | bytes 6148
  96.5 5.0 %copy-start.21 = (f32[512]{0:T(512)}, f32[512]{0:T(512)S(1)}, u32[]{:S(2)}) copy-start(f32[512]{0:T(512)S(1)} %get-tuple-element.111) | copy-start | bytes 6148
  96.6 5.0 %copy-start.23 = (f32[512]{0:T(512)}, f32[512]{0:T(512)S(1)}, u32[]{:S(2)}) copy-start(f32[512]{0:T(512)S(1)} %get-tuple-element.112) | copy-start | bytes 6148
  96.6 5.0 %copy-start.25 = (f32[512]{0:T(512)}, f32[512]{0:T(512)S(1)}, u32[]{:S(2)}) copy-start(f32[512]{0:T(512)S(1)} %get-tuple-element.113) | copy-start | bytes 6148
  96.6 5.0 %copy-start.27 = (f32[512]{0:T(512)}, f32[512]{0:T(512)S(1)}, u32[]{:S(2)}) copy-start(f32[512]{0:T(512)S(1)} %get-tuple-element.114) | copy-start | bytes 6148
  96.6 5.0 %copy-start.29 = (f32[512]{0:T(512)}, f32[512]{0:T(512)S(1)}, u32[]{:S(2)}) copy-start(f32[512]{0:T(512)S(1)} %get-tuple-element.115) | copy-start | bytes 6148
  96.6 5.0 %copy-start.31 = (f32[512]{0:T(512)}, f32[512]{0:T(512)S(1)}, u32[]{:S(2)}) copy-start(f32[512]{0:T(512)S(1)} %get-tuple-element.116) | copy-start | bytes 6148
  96.6 5.0 %copy-start.33 = (f32[512]{0:T(512)}, f32[512]{0:T(512)S(1)}, u32[]{:S(2)}) copy-start(f32[512]{0:T(512)S(1)} %get-tuple-element.117) | copy-start | bytes 6148
  123.5 130.7 %reduce-scatter.6.cloned.1.call-start = ((), (), s32[]{:S(2)}) async-start(), calls=%async_computation.5 | async-start | bytes 4456448 | tf_op jit(solution)/shard_map/reduce_scatter | solution.py:124
  127.7 202.6 %reduce-scatter.8.cloned.1.call-start = ((), (), s32[]{:S(2)}) async-start(), calls=%async_computation.6 | async-start | bytes 4456448 | tf_op jit(solution)/shard_map/reduce_scatter | solution.py:115
  194.5 6.6 %collective-permute-start.2 = (bf16[3,64,512]{2,1,0:T(8,128)(2,1)S(1)}, bf16[3,64,512]{2,1,0:T(8,128)(2,1)S(1)}, u32[]{:S(2)}, u32[]{:S(2)}) collective-permute-start(bf16[3,64,512]{2,1,0:T(8,128)(2,1)S(1)} %get-tuple-element.145), channel_id=1, source_target_pairs={{0,1},{1,2},{2,3},{3,4},{4,5},{5,6},{6,7},{7,8},{8,9},{9,10},{10,1... | collective-permute-start | bytes 589832 | tf_op jit(solution)/shard_map/ppermute | solution.py:15
  195.8 5.3 %collective-permute-start.3 = (bf16[3,64,512]{2,1,0:T(8,128)(2,1)S(1)}, bf16[3,64,512]{2,1,0:T(8,128)(2,1)S(1)}, u32[]{:S(2)}, u32[]{:S(2)}) collective-permute-start(bf16[3,64,512]{2,1,0:T(8,128)(2,1)S(1)} %get-tuple-element.146), channel_id=1, source_target_pairs={{1,0},{2,1},{3,2},{4,3},{5,4},{6,5},{7,6},{8,7},{9,8},{10,9},{11,1... | collective-permute-start | bytes 589832 | tf_op jit(solution)/shard_map/ppermute | solution.py:18
  (55 other events, 101.3 us)
Sparse Core Ops, SparseCore 0:
  10.1 44.2 all-gather.3
  56.6 40.1 all-gather.5
  123.6 54.3 reduce-scatter.9
  182.2 71.8 reduce-scatter.5
  258.4 71.7 reduce-scatter.7
where the time goes:
time: 337 us
  blocking collectives  133 us (39%)
  waiting for transfers between devices  126 us (37%)
  matrix products  18.4 us (5%)
  local copies, waits for them, and re-layouts  18.3 us (5%)
  other arithmetic  17.8 us (5%)
  between operations  16.9 us (5%)
  starting transfers between devices  6.71 us (2%)
    unnamed x2, blocking collectives  89.8 us
    reduce_scatter x1, waiting for transfers between devices, per_device(): lax.psum_scatter(down_full, 'row', scatter_dimension=0, tiled=True)  76.1 us
    reduce_scatter x1, waiting for transfers between devices, per_device(): lax.psum_scatter(lax.dot_general(columns, dhidden, (((0,), (0,)), ((), ()...  48.2 us
    all_gather x1, blocking collectives, per_device(): lax.all_gather(depth_weight, 'row', axis=1, tiled=True)  25.6 us
    all_gather x1, blocking collectives, per_device(): lax.all_gather(up_bias, 'row', axis=0, tiled=True)  17.5 us
    unnamed x155, local copies, waits for them, and re-layouts  7.34 us
    slice x3, local copies, waits for them, and re-layouts, depth_conv(): kernel[first * 7 + second]  6.92 us
  transfers between devices with their start and end apart: 9, of which 2 were waited for; matrix products, arithmetic and copies ran while one was open for 11% of the time, Pallas kernels for 0%

commit v1 on v0

--- a/solution.py
+++ b/solution.py
@@ -5,6 +5,24 @@
 from jax.sharding import PartitionSpec as P
 
 eps = 1e-06
+
+
+def gather_around(shard, axis, dim):
+    ways, here, step = (lax.axis_size(axis), lax.axis_index(axis), shard.shape[dim])
+    shape = [n * ways if d == dim else n for d, n in enumerate(shard.shape)]
+    full = lax.dynamic_update_slice_in_dim(
+        jnp.zeros(shape, shard.dtype), shard, here * step, axis=dim
+    )
+    going_up = going_down = shard
+    for far in range(1, ways // 2 + 1):
+        going_up = lax.ppermute(going_up, axis, [(d, (d + 1) % ways) for d in range(ways)])
+        full = lax.dynamic_update_slice_in_dim(full, going_up, (here - far) % ways * step, axis=dim)
+        if 2 * far < ways:
+            going_down = lax.ppermute(going_down, axis, [(d, (d - 1) % ways) for d in range(ways)])
+            full = lax.dynamic_update_slice_in_dim(
+                full, going_down, (here + far) % ways * step, axis=dim
+            )
+    return full
 
 
 def with_halo(block, sides, width):
@@ -76,7 +94,7 @@
         lax.all_gather(norm_gain, "row", axis=0, tiled=True),
         lax.all_gather(norm_shift, "row", axis=0, tiled=True),
         lax.all_gather(down_bias, "row", axis=0, tiled=True),
-        lax.all_gather(up_bias, "row", axis=0, tiled=True),
+        gather_around(up_bias, "row", 0),
     )
     kernel = kernel.astype(jnp.float32)
     gain = gain.astype(jnp.float32)

time: 337 us -> 360 us (1.068)
  starting transfers between devices: 6.71 us -> 37.7 us
  blocking collectives: 133 us -> 111 us
  waiting for transfers between devices: 126 us -> 136 us
    ppermute x0 -> x15, starting transfers between devices: none -> 32.1 us  [the longest x7 31.5 us: gather_around(): lax.ppermute(going_down, axis, [(d, (d - 1) % ways) for d in range(ways)])]
    all_gather x1 -> x0, blocking collectives: 17.5 us -> none  [per_device(): lax.all_gather(up_bias, 'row', axis=0, tiled=True)]
    ppermute x0 -> x15, waiting for transfers between devices: none -> 10.4 us  [the longest x8 10.1 us: gather_around(): lax.ppermute(going_up, axis, [(d, (d + 1) % ways) for d in range(ways)])]
  transfers between devices with their start and end apart: 9 -> 24, of which waited for: 2 -> 13; matrix products, arithmetic and copies ran while one was open for 11% -> 11% of each run, Pallas kernels for 0% -> 0%
where the time goes in v1:
time: 360 us
  waiting for transfers between devices  136 us (38%)
  blocking collectives  111 us (31%)
  starting transfers between devices  37.7 us (10%)
  local copies, waits for them, and re-layouts  21.4 us (6%)
  matrix products  18.4 us (5%)
  other arithmetic  17.8 us (5%)
  between operations  17.2 us (5%)
    unnamed x2, blocking collectives  88.2 us
    reduce_scatter x1, waiting for transfers between devices, per_device(): lax.psum_scatter(down_full, 'row', scatter_dimension=0, tiled=True)  76 us
    reduce_scatter x1, waiting for transfers between devices, per_device(): lax.psum_scatter(lax.dot_general(columns, dhidden, (((0,), (0,)), ((), ()...  48.3 us
    ppermute x7, starting transfers between devices, gather_around(): lax.ppermute(going_down, axis, [(d, (d - 1) % ways) for d in range(ways)])  31.5 us
    all_gather x1, blocking collectives, per_device(): lax.all_gather(depth_weight, 'row', axis=1, tiled=True)  23 us
    ppermute x8, waiting for transfers between devices, gather_around(): lax.ppermute(going_up, axis, [(d, (d + 1) % ways) for d in range(ways)])  10.1 us
    unnamed x155, local copies, waits for them, and re-layouts  7.34 us
  transfers between devices with their start and end apart: 24, of which 13 were waited for; matrix products, arithmetic and copies ran while one was open for 11% of the time, Pallas kernels for 0%

profile of v1, /device:TPU:0, one launch (start us, length us, event | category | flops | bytes accessed | tf_op | source)
XLA Modules:
  0.0 359.8 jit_solution(12890754750236040812)
XLA Ops:
  9.2 5.0 %collective-permute-start.3 = (bf16[128]{0:T(256)(128)(2,1)}, bf16[128]{0:T(256)(128)(2,1)S(1)}, u32[]{:S(2)}, u32[]{:S(2)}) collective-permute-start(bf16[128]{0:T(256)(128)(2,1)} %param.17), channel_id=1, source_target_pairs={{0,15},{1,0},{2,1},{3,2},{4,3},{5,4},{6,5},{7,6},{8,7},{9,8},{10,9... | collective-permute-start | bytes 776 | tf_op jit(solution)/shard_map/ppermute | solution.py:21
  18.0 23.0 %all_gather.23 = bf16[49,512]{0,1:T(8,128)(2,1)S(1)} all-gather(bf16[49,32]{0,1:T(8,128)(2,1)} %param.12), channel_id=1, replica_groups=mesh['groups'=2,'row'=16] {'row'}, dimensions={1}, use_global_device_ids=true | all-gather | bytes 53312 | tf_op jit(solution)/shard_map/all_gather | solution.py:92
  41.0 2.6 slice_reduce_fusion.48
  47.8 30.5 %all-reduce.12 = (bf16[512]{0:T(512)(128)(2,1)S(1)}, bf16[512]{0:T(512)(128)(2,1)S(1)}, bf16[512]{0:T(512)(128)(2,1)S(1)}, bf16[512]{0:T(512)(128)(2,1)}) all-reduce(bf16[512]{0:T(512)(128)(2,1)S(1)} %dynamic-update-slice, bf16[512]{0:T(512)(128)(2,1)S(1)} %dynamic-update-slice.2, ...), channel_id=1, replica_groups=mesh['groups'=2,'row'=16] {'row'}, use_global_device_ids=true, to_apply=%add.2 | all-reduce | flops 2048 | bytes 8192
  78.3 2.7 slice_reduce_fusion.47
  81.3 4.4 %collective-permute-start.5 = (bf16[128]{0:T(256)(128)(2,1)S(1)}, bf16[128]{0:T(256)(128)(2,1)S(1)}, u32[]{:S(2)}, u32[]{:S(2)}) collective-permute-start(bf16[128]{0:T(256)(128)(2,1)S(1)} %collective-permute-done.3), channel_id=1, source_target_pairs={{0,15},{1,0},{2,1},{3,2},{4,3},{5,4},{6,5},{7,6},{8,7},{9,8},{10,9... | collective-permute-start | bytes 776 | tf_op jit(solution)/shard_map/ppermute | solution.py:21
  87.3 4.4 %collective-permute-start.7 = (bf16[128]{0:T(256)(128)(2,1)S(1)}, bf16[128]{0:T(256)(128)(2,1)S(1)}, u32[]{:S(2)}, u32[]{:S(2)}) collective-permute-start(bf16[128]{0:T(256)(128)(2,1)S(1)} %collective-permute-done.5), channel_id=1, source_target_pairs={{0,15},{1,0},{2,1},{3,2},{4,3},{5,4},{6,5},{7,6},{8,7},{9,8},{10,9... | collective-permute-start | bytes 776 | tf_op jit(solution)/shard_map/ppermute | solution.py:21
  93.0 4.4 %collective-permute-start.9 = (bf16[128]{0:T(256)(128)(2,1)S(1)}, bf16[128]{0:T(256)(128)(2,1)S(1)}, u32[]{:S(2)}, u32[]{:S(2)}) collective-permute-start(bf16[128]{0:T(256)(128)(2,1)S(1)} %collective-permute-done.7), channel_id=1, source_target_pairs={{0,15},{1,0},{2,1},{3,2},{4,3},{5,4},{6,5},{7,6},{8,7},{9,8},{10,9... | collective-permute-start | bytes 776 | tf_op jit(solution)/shard_map/ppermute | solution.py:21
  99.0 4.5 %collective-permute-start.11 = (bf16[128]{0:T(256)(128)(2,1)S(1)}, bf16[128]{0:T(256)(128)(2,1)S(1)}, u32[]{:S(2)}, u32[]{:S(2)}) collective-permute-start(bf16[128]{0:T(256)(128)(2,1)S(1)} %collective-permute-done.9), channel_id=1, source_target_pairs={{0,15},{1,0},{2,1},{3,2},{4,3},{5,4},{6,5},{7,6},{8,7},{9,8},{10,9... | collective-permute-start | bytes 776 | tf_op jit(solution)/shard_map/ppermute | solution.py:21
  104.7 4.4 %collective-permute-start.13 = (bf16[128]{0:T(256)(128)(2,1)S(1)}, bf16[128]{0:T(256)(128)(2,1)S(1)}, u32[]{:S(2)}, u32[]{:S(2)}) collective-permute-start(bf16[128]{0:T(256)(128)(2,1)S(1)} %collective-permute-done.11), channel_id=1, source_target_pairs={{0,15},{1,0},{2,1},{3,2},{4,3},{5,4},{6,5},{7,6},{8,7},{9,8},{10,9... | collective-permute-start | bytes 776 | tf_op jit(solution)/shard_map/ppermute | solution.py:21
  110.4 4.4 %collective-permute-start.15 = (bf16[128]{0:T(256)(128)(2,1)S(1)}, bf16[128]{0:T(256)(128)(2,1)S(1)}, u32[]{:S(2)}, u32[]{:S(2)}) collective-permute-start(bf16[128]{0:T(256)(128)(2,1)S(1)} %collective-permute-done.13), channel_id=1, source_target_pairs={{0,15},{1,0},{2,1},{3,2},{4,3},{5,4},{6,5},{7,6},{8,7},{9,8},{10,9... | collective-permute-start | bytes 776 | tf_op jit(solution)/shard_map/ppermute | solution.py:21
  116.3 4.9 %collective-permute-done.16 = bf16[128]{0:T(256)(128)(2,1)S(1)} collective-permute-done((bf16[128]{0:T(256)(128)(2,1)S(1)}, bf16[128]{0:T(256)(128)(2,1)S(1)}, u32[]{:S(2)}, u32[]{:S(2)}) %collective-permute-start.16) | collective-permute-done | bytes 288 | tf_op jit(solution)/shard_map/ppermute | solution.py:18
  121.4 4.7 %fusion.146 = (f32[4,64]{1,0:T(4,128)S(1)}, f32[4,64,512]{2,1,0:T(8,128)S(1)}) fusion(f32[512]{0:T(512)S(1)} %convert_element_type.62, f32[512]{0:T(512)S(1)} %get-tuple-element.85, f32[512]{0:T(512)S(1)} %get-tuple-element.86, f32[512]{0:T(512)S(1)} %get-tuple-element.87, f32[512]{0:T(512)S(1)} %get-tuple-element.88, ...), kind=kLoop, calls=%fused_computation.367 | loop fusion | flops 12975872 | bytes 5608448 | tf_op jit(solution)/shard_map/reduce_sum | solution.py:104
  126.8 3.8 %multiply_convert_fusion = (bf16[256,2048]{1,0:T(8,128)(2,1)S(1)}, f32[256,2048]{1,0:T(8,128)}) fusion(f32[2048]{0:T(1024)S(1)} %convert_element_type.66, bf16[256,512]{1,0:T(8,128)(2,1)S(1)} %bitcast.73, bf16[512,2048]{1,0:T(8,128)(2,1)} %all-gather.3.cloned.1.call-done), kind=kOutput, calls=%fused_computation.60 | convolution fusion | flops 540016640 | bytes 5513216 | tf_op jit(solution)/shard_map/dot_general | solution.py:113
  130.5 4.3 %convert_reduce_fusion.1 = (f32[2048]{0:T(1024)}, bf16[256,2048]{1,0:T(8,128)(2,1)S(1)}) fusion(f32[256,2048]{1,0:T(8,128)} %get-tuple-element.152, f32[2048]{0:T(1024)S(1)} %convert_element_type.66, bf16[256,512]{1,0:T(8,128)(2,1)} %bitcast.75, bf16[2048,512]{1,0:T(8,128)(2,1)} %all-gather.5.cloned.1.call-done), kind=kOutput, calls=%fused_computation.59 | convolution fusion | flops 543684608 | bytes 5521408 | tf_op jit(solution)/shard_map/dot_general | solution.py:134
  139.1 3.2 fusion.143
  145.0 2.3 stack.199
  148.4 3.9 %convolution_multiply_fusion.1 = f32[512,2048]{1,0:T(8,128)} fusion(bf16[256,512]{1,0:T(8,128)(2,1)S(1)} %bitcast.74, bf16[256,2048]{1,0:T(8,128)(2,1)} %copy-done.6), kind=kOutput, calls=%fused_computation.51 | convolution fusion | flops 537919488 | bytes 5505024 | tf_op jit(solution)/shard_map/dot_general | solution.py:143
  153.3 2.7 convolution_multiply_fusion
  157.5 57.6 %all-reduce.11 = (f32[512]{0:T(512)S(1)}, f32[512]{0:T(512)S(1)}, f32[512]{0:T(512)S(1)}, f32[2048]{0:T(1024)S(1)}, f32[512]{0:T(512)S(1)}) all-reduce(f32[512]{0:T(512)S(1)} %broadcast_multiply_fusion.5, f32[512]{0:T(512)S(1)} %get-tuple-element.157, ...), channel_id=5, replica_groups=mesh['groups'=2,'row'=16] {'row'}, use_global_device_ids=true, to_apply=%region_57.58.clone | all-reduce | flops 4096 | bytes 32768
  220.7 2.4 convolution_add_fusion
  224.3 4.7 %fusion.5 = bf16[4,64,512]{2,1,0:T(8,128)(2,1)} fusion(bf16[4,64,512]{2,1,0:T(8,128)(2,1)S(1)} %copy-done.4, f32[10,64,512]{2,1,0:T(8,128)S(1)} %maximum_convert_fusion.1, f32[512]{0:T(512)S(1)} %get-tuple-element.85, f32[512]{0:T(512)S(1)} %get-tuple-element.86, f32[512]{0:T(512)S(1)} %get-tuple-element.87, f32[512]{0:T(512)S(1)} %get-tuple-element.88, ...), kind=kLoop, calls=%fused_computation.151 | loop fusion | flops 13107200 | bytes 5605376 | tf_op jit(solution)/shard_map/convert_element_type | solution.py:180
  229.0 48.3 %reduce-scatter.6.cloned.1.call-done = f32[32,2048]{1,0:T(8,128)} async-done(((f32[512,2048]{1,0:T(8,128)}), f32[32,2048]{1,0:T(8,128)}) %reduce-scatter.6.cloned.1.call-update) | async-done | bytes 262160 | tf_op jit(solution)/shard_map/reduce_scatter | solution.py:142
  277.3 76.0 %reduce-scatter.8.cloned.1.call-done = f32[128,512]{1,0:T(8,128)} async-done(((f32[2048,512]{1,0:T(8,128)}), f32[128,512]{1,0:T(8,128)}) %reduce-scatter.8.cloned.1.call-update) | async-done | bytes 262160 | tf_op jit(solution)/shard_map/reduce_scatter | solution.py:133
  (244 shorter events, 33.7 us)
Async XLA Ops:
  7.2 119.6 %all-gather.3.cloned.1.call-start = ((), (), s32[]{:S(2)}) async-start(), calls=%async_computation.3 | async-start | bytes 2228224 | tf_op jit(solution)/shard_map/all_gather | solution.py:115
  7.9 122.6 %all-gather.5.cloned.1.call-start = ((), (), s32[]{:S(2)}) async-start(), calls=%async_computation.4 | async-start | bytes 2228224 | tf_op jit(solution)/shard_map/all_gather | solution.py:122
  8.7 220.3 %reduce-scatter.10.cloned.1.call-start = ((), (), s32[]{:S(2)}) async-start(), calls=%async_computation.7 | async-start | bytes 278528
  8.7 72.5 %collective-permute-start.2 = (bf16[128]{0:T(256)(128)(2,1)}, bf16[128]{0:T(256)(128)(2,1)S(1)}, u32[]{:S(2)}, u32[]{:S(2)}) collective-permute-start(bf16[128]{0:T(256)(128)(2,1)} %param.17), channel_id=1, source_target_pairs={{0,1},{1,2},{2,3},{3,4},{4,5},{5,6},{6,7},{7,8},{8,9},{9,10},{10,1... | collective-permute-start | bytes 776 | tf_op jit(solution)/shard_map/ppermute | solution.py:18
  9.2 72.0 %collective-permute-start.3 = (bf16[128]{0:T(256)(128)(2,1)}, bf16[128]{0:T(256)(128)(2,1)S(1)}, u32[]{:S(2)}, u32[]{:S(2)}) collective-permute-start(bf16[128]{0:T(256)(128)(2,1)} %param.17), channel_id=1, source_target_pairs={{0,15},{1,0},{2,1},{3,2},{4,3},{5,4},{6,5},{7,6},{8,7},{9,8},{10,9... | collective-permute-start | bytes 776 | tf_op jit(solution)/shard_map/ppermute | solution.py:21
  15.3 106.0 %collective-permute-start = (bf16[3,64,512]{2,1,0:T(8,128)(2,1)S(1)}, bf16[3,64,512]{2,1,0:T(8,128)(2,1)S(1)}, u32[]{:S(2)}, u32[]{:S(2)}) collective-permute-start(bf16[3,64,512]{2,1,0:T(8,128)(2,1)S(1)} %get-tuple-element.147), channel_id=1, source_target_pairs={{0,1},{1,2},{2,3},{3,4},{4,5},{5,6},{6,7},{7,8},{8,9},{9,10},{10,1... | collective-permute-start | bytes 589832 | tf_op jit(solution)/shard_map/ppermute | solution.py:33
  16.7 104.7 %collective-permute-start.1 = (bf16[3,64,512]{2,1,0:T(8,128)(2,1)S(1)}, bf16[3,64,512]{2,1,0:T(8,128)(2,1)S(1)}, u32[]{:S(2)}, u32[]{:S(2)}) collective-permute-start(bf16[3,64,512]{2,1,0:T(8,128)(2,1)S(1)} %get-tuple-element.148), channel_id=1, source_target_pairs={{1,0},{2,1},{3,2},{4,3},{5,4},{6,5},{7,6},{8,7},{9,8},{10,9},{11,1... | collective-permute-start | bytes 589832 | tf_op jit(solution)/shard_map/ppermute | solution.py:36
  81.2 5.8 %collective-permute-start.4 = (bf16[128]{0:T(256)(128)(2,1)S(1)}, bf16[128]{0:T(256)(128)(2,1)S(1)}, u32[]{:S(2)}, u32[]{:S(2)}) collective-permute-start(bf16[128]{0:T(256)(128)(2,1)S(1)} %collective-permute-done.2), channel_id=1, source_target_pairs={{0,1},{1,2},{2,3},{3,4},{4,5},{5,6},{6,7},{7,8},{8,9},{9,10},{10,1... | collective-permute-start | bytes 776 | tf_op jit(solution)/shard_map/ppermute | solution.py:18
  81.3 5.9 %collective-permute-start.5 = (bf16[128]{0:T(256)(128)(2,1)S(1)}, bf16[128]{0:T(256)(128)(2,1)S(1)}, u32[]{:S(2)}, u32[]{:S(2)}) collective-permute-start(bf16[128]{0:T(256)(128)(2,1)S(1)} %collective-permute-done.3), channel_id=1, source_target_pairs={{0,15},{1,0},{2,1},{3,2},{4,3},{5,4},{6,5},{7,6},{8,7},{9,8},{10,9... | collective-permute-start | bytes 776 | tf_op jit(solution)/shard_map/ppermute | solution.py:21
  87.0 5.7 %collective-permute-start.6 = (bf16[128]{0:T(256)(128)(2,1)S(1)}, bf16[128]{0:T(256)(128)(2,1)S(1)}, u32[]{:S(2)}, u32[]{:S(2)}) collective-permute-start(bf16[128]{0:T(256)(128)(2,1)S(1)} %collective-permute-done.4), channel_id=1, source_target_pairs={{0,1},{1,2},{2,3},{3,4},{4,5},{5,6},{6,7},{7,8},{8,9},{9,10},{10,1... | collective-permute-start | bytes 776 | tf_op jit(solution)/shard_map/ppermute | solution.py:18
  87.3 5.7 %collective-permute-start.7 = (bf16[128]{0:T(256)(128)(2,1)S(1)}, bf16[128]{0:T(256)(128)(2,1)S(1)}, u32[]{:S(2)}, u32[]{:S(2)}) collective-permute-start(bf16[128]{0:T(256)(128)(2,1)S(1)} %collective-permute-done.5), channel_id=1, source_target_pairs={{0,15},{1,0},{2,1},{3,2},{4,3},{5,4},{6,5},{7,6},{8,7},{9,8},{10,9... | collective-permute-start | bytes 776 | tf_op jit(solution)/shard_map/ppermute | solution.py:21
  92.7 5.7 %collective-permute-start.8 = (bf16[128]{0:T(256)(128)(2,1)S(1)}, bf16[128]{0:T(256)(128)(2,1)S(1)}, u32[]{:S(2)}, u32[]{:S(2)}) collective-permute-start(bf16[128]{0:T(256)(128)(2,1)S(1)} %collective-permute-done.6), channel_id=1, source_target_pairs={{0,1},{1,2},{2,3},{3,4},{4,5},{5,6},{6,7},{7,8},{8,9},{9,10},{10,1... | collective-permute-start | bytes 776 | tf_op jit(solution)/shard_map/ppermute | solution.py:18
  93.0 6.0 %collective-permute-start.9 = (bf16[128]{0:T(256)(128)(2,1)S(1)}, bf16[128]{0:T(256)(128)(2,1)S(1)}, u32[]{:S(2)}, u32[]{:S(2)}) collective-permute-start(bf16[128]{0:T(256)(128)(2,1)S(1)} %collective-permute-done.7), channel_id=1, source_target_pairs={{0,15},{1,0},{2,1},{3,2},{4,3},{5,4},{6,5},{7,6},{8,7},{9,8},{10,9... | collective-permute-start | bytes 776 | tf_op jit(solution)/shard_map/ppermute | solution.py:21
  98.4 5.7 %collective-permute-start.10 = (bf16[128]{0:T(256)(128)(2,1)S(1)}, bf16[128]{0:T(256)(128)(2,1)S(1)}, u32[]{:S(2)}, u32[]{:S(2)}) collective-permute-start(bf16[128]{0:T(256)(128)(2,1)S(1)} %collective-permute-done.8), channel_id=1, source_target_pairs={{0,1},{1,2},{2,3},{3,4},{4,5},{5,6},{6,7},{7,8},{8,9},{9,10},{10,1... | collective-permute-start | bytes 776 | tf_op jit(solution)/shard_map/ppermute | solution.py:18
  99.0 5.8 %collective-permute-start.11 = (bf16[128]{0:T(256)(128)(2,1)S(1)}, bf16[128]{0:T(256)(128)(2,1)S(1)}, u32[]{:S(2)}, u32[]{:S(2)}) collective-permute-start(bf16[128]{0:T(256)(128)(2,1)S(1)} %collective-permute-done.9), channel_id=1, source_target_pairs={{0,15},{1,0},{2,1},{3,2},{4,3},{5,4},{6,5},{7,6},{8,7},{9,8},{10,9... | collective-permute-start | bytes 776 | tf_op jit(solution)/shard_map/ppermute | solution.py:21
  104.1 5.7 %collective-permute-start.12 = (bf16[128]{0:T(256)(128)(2,1)S(1)}, bf16[128]{0:T(256)(128)(2,1)S(1)}, u32[]{:S(2)}, u32[]{:S(2)}) collective-permute-start(bf16[128]{0:T(256)(128)(2,1)S(1)} %collective-permute-done.10), channel_id=1, source_target_pairs={{0,1},{1,2},{2,3},{3,4},{4,5},{5,6},{6,7},{7,8},{8,9},{9,10},{10,1... | collective-permute-start | bytes 776 | tf_op jit(solution)/shard_map/ppermute | solution.py:18
  104.7 5.7 %collective-permute-start.13 = (bf16[128]{0:T(256)(128)(2,1)S(1)}, bf16[128]{0:T(256)(128)(2,1)S(1)}, u32[]{:S(2)}, u32[]{:S(2)}) collective-permute-start(bf16[128]{0:T(256)(128)(2,1)S(1)} %collective-permute-done.11), channel_id=1, source_target_pairs={{0,15},{1,0},{2,1},{3,2},{4,3},{5,4},{6,5},{7,6},{8,7},{9,8},{10,9... | collective-permute-start | bytes 776 | tf_op jit(solution)/shard_map/ppermute | solution.py:21
  109.8 5.7 %collective-permute-start.14 = (bf16[128]{0:T(256)(128)(2,1)S(1)}, bf16[128]{0:T(256)(128)(2,1)S(1)}, u32[]{:S(2)}, u32[]{:S(2)}) collective-permute-start(bf16[128]{0:T(256)(128)(2,1)S(1)} %collective-permute-done.12), channel_id=1, source_target_pairs={{0,1},{1,2},{2,3},{3,4},{4,5},{5,6},{6,7},{7,8},{8,9},{9,10},{10,1... | collective-permute-start | bytes 776 | tf_op jit(solution)/shard_map/ppermute | solution.py:18
  110.4 5.7 %collective-permute-start.15 = (bf16[128]{0:T(256)(128)(2,1)S(1)}, bf16[128]{0:T(256)(128)(2,1)S(1)}, u32[]{:S(2)}, u32[]{:S(2)}) collective-permute-start(bf16[128]{0:T(256)(128)(2,1)S(1)} %collective-permute-done.13), channel_id=1, source_target_pairs={{0,15},{1,0},{2,1},{3,2},{4,3},{5,4},{6,5},{7,6},{8,7},{9,8},{10,9... | collective-permute-start | bytes 776 | tf_op jit(solution)/shard_map/ppermute | solution.py:21
  115.4 5.7 %collective-permute-start.16 = (bf16[128]{0:T(256)(128)(2,1)S(1)}, bf16[128]{0:T(256)(128)(2,1)S(1)}, u32[]{:S(2)}, u32[]{:S(2)}) collective-permute-start(bf16[128]{0:T(256)(128)(2,1)S(1)} %collective-permute-done.14), channel_id=1, source_target_pairs={{0,1},{1,2},{2,3},{3,4},{4,5},{5,6},{6,7},{7,8},{8,9},{9,10},{10,1... | collective-permute-start | bytes 776 | tf_op jit(solution)/shard_map/ppermute | solution.py:18
  148.2 129.1 %reduce-scatter.6.cloned.1.call-start = ((), (), s32[]{:S(2)}) async-start(), calls=%async_computation.5 | async-start | bytes 4456448 | tf_op jit(solution)/shard_map/reduce_scatter | solution.py:142
  152.3 200.9 %reduce-scatter.8.cloned.1.call-start = ((), (), s32[]{:S(2)}) async-start(), calls=%async_computation.6 | async-start | bytes 4456448 | tf_op jit(solution)/shard_map/reduce_scatter | solution.py:133
  217.5 6.6 %collective-permute-start.17 = (bf16[3,64,512]{2,1,0:T(8,128)(2,1)S(1)}, bf16[3,64,512]{2,1,0:T(8,128)(2,1)S(1)}, u32[]{:S(2)}, u32[]{:S(2)}) collective-permute-start(bf16[3,64,512]{2,1,0:T(8,128)(2,1)S(1)} %get-tuple-element.145), channel_id=1, source_target_pairs={{0,1},{1,2},{2,3},{3,4},{4,5},{5,6},{6,7},{7,8},{8,9},{9,10},{10,1... | collective-permute-start | bytes 589832 | tf_op jit(solution)/shard_map/ppermute | solution.py:33
  218.8 5.2 %collective-permute-start.18 = (bf16[3,64,512]{2,1,0:T(8,128)(2,1)S(1)}, bf16[3,64,512]{2,1,0:T(8,128)(2,1)S(1)}, u32[]{:S(2)}, u32[]{:S(2)}) collective-permute-start(bf16[3,64,512]{2,1,0:T(8,128)(2,1)S(1)} %get-tuple-element.146), channel_id=1, source_target_pairs={{1,0},{2,1},{3,2},{4,3},{5,4},{6,5},{7,6},{8,7},{9,8},{10,9},{11,1... | collective-permute-start | bytes 589832 | tf_op jit(solution)/shard_map/ppermute | solution.py:36
  (70 other events, 944.1 us)
Sparse Core Ops, SparseCore 0:
  10.1 44.7 all-gather.2
  57.1 40.2 all-gather.4
  148.3 52.8 reduce-scatter.9
  205.4 71.7 reduce-scatter.5
  281.6 71.6 reduce-scatter.7
